TPU v7x, 32 devices: a whole 2x2x4 slice. The times are simulated.
32 devices in a mesh: section: 4 (over y, x), dp: 4 (over z), mp: 2 (over core).
Axes of the slice: x: 2, y: 2, z: 4, core: 2. Of those that a mesh axis runs over, the one named last changes fastest.
Arguments:
- encoded: float32 [8, 64, 4096], P('dp', None, ('section', 'mp')), may hold values from -6 to 6
- counts: int32 [8], replicated, may hold values from 1 to 64, 384 in all
- owner: int32 [8], replicated, may hold values from 0 to 3, as said below
- w_key: bfloat16 [4, 4096, 2048], P('section', 'dp', 'mp'), may hold values from -0.09375 to 0.09375
- w_value: bfloat16 [4, 4096, 2048], P('section', 'dp', 'mp'), may hold values from -0.09375 to 0.09375
- queries: bfloat16 [4, 16, 128, 2048], P('section', 'dp', None, 'mp'), may hold values from -6 to 6
- grad_out: bfloat16 [4, 16, 128, 2048], P('section', 'dp', None, 'mp'), may hold values from -6 to 6
- dec_mask: int32 [16, 128], P('dp'), may hold values 0 or 1
Outputs:
- attn_out: bfloat16 [4, 16, 128, 2048], P('section', 'dp', None, 'mp')
- d_encoded: float32 [8, 64, 4096], P('dp', None, ('section', 'mp'))
Inputs may be any that keep to these rules, and one draw needn't show every extreme that they name: Each owner holds at most 4 dialogues and some owner holds exactly 4.
All inputs are finite; a program needn't handle non-finite values. No bound on the sum of `dec_mask` on one device may be relied on, other than what follows from the above.
Results may differ from a plain program's by a relative error of at most 0.014.
Values may be sent and summed in bfloat16 or wider, within the bound.
A program may use at most 128 MiB of HBM per device.

v0:
```python
import functools

import jax
import jax.numpy as jnp
from jax import lax
from jax.experimental import pallas as pl
from jax.experimental.pallas import tpu as pltpu
from jax.sharding import PartitionSpec as P

HEAD_DIM = 256
MESH = pl.DeviceIdType.MESH
F32 = jnp.float32
BF16 = jnp.bfloat16


def skew(hops):
    return (5 * hops + 2) // 3


def lag_of(groups):
    return pl.cdiv(groups - 1 + skew(groups - 1), groups) * groups


def dot(left, right, left_dim, right_dim):
    return lax.dot_general(
        left, right, (((left_dim,), (right_dim,)), ((), ())), preferred_element_type=F32
    )


def kernel(
    dims,
    counts,
    owner,
    encoded,
    w_key,
    w_value,
    queries,
    grad_out,
    mask,
    attn_out,
    d_encoded,
    table,
    weights,
    enc_cast,
    enc_all,
    part,
    recv,
    send,
    own_grad,
    acc,
    d_send,
    d_pair,
    d_mid,
    d_recv,
    d_fin,
    d_arrived,
    w_sem,
    swap_send,
    swap_recv,
    self_sem,
    enc_send_sem,
    enc_pass_sem,
    enc_recv_sem,
    send_sem,
    recv_sem,
    pair_send_sem,
    pair_recv_sem,
    d_send_sem,
    d_recv_sem,
):
    sections, groups, cores = dims
    section = lax.axis_index("section")
    p = lax.axis_index("dp")
    core = lax.axis_index("mp")
    fold = sections // groups
    local_count, key_len, feat = encoded.shape
    dialogs = local_count * groups
    block_rows = local_count * key_len
    cap = queries.shape[0]
    heads = queries.shape[2] // HEAD_DIM
    per = local_count
    subs = groups
    pieces = heads * subs
    lag = lag_of(groups)
    late = skew(groups - 1)
    others = cores - 1
    scale = HEAD_DIM ** (-0.5)

    swap_section, swap_p = p * fold + lax.rem(section, fold), section // fold
    stays = section // fold == p

    def region(s, m):
        rows = pl.multiple_of((s // fold) * block_rows, block_rows)
        cols = pl.multiple_of((lax.rem(s, fold) * cores + m) * feat, feat)
        return pl.ds(rows, block_rows), pl.ds(cols, feat)

    def remote(src, dst, out_sem, in_sem, device):
        return pltpu.make_async_remote_copy(
            src_ref=src,
            dst_ref=dst,
            send_sem=out_sem,
            recv_sem=in_sem,
            device_id=device,
            device_id_type=MESH,
        )

    barrier = pltpu.get_barrier_semaphore()

    def greet(s, z, m):
        pl.semaphore_signal(barrier, inc=1, device_id=(s, z, m), device_id_type=MESH)

    @pl.when(jnp.logical_not(stays))
    def _():
        greet(swap_section, swap_p, core)

    @pl.when(p > 0)
    def _():
        greet(section, p - 1, core)

    @pl.when(p < groups - 1)
    def _():
        greet(section, p + 1, core)

    @pl.loop(1, sections)
    def _(i):
        greet(lax.rem(section + i, sections), p, core)

    for j in range(1, cores):
        greet(section, p, lax.rem(core + j, cores))

    copies = []
    for h in range(heads):
        for kv, ref in enumerate((w_key, w_value)):
            copy = pltpu.make_async_copy(
                ref.at[:, pl.ds(h * HEAD_DIM, HEAD_DIM)],
                weights.at[2 * h + kv],
                w_sem.at[2 * h + kv],
            )
            copy.start()
            copies.append(copy)

    for a in range(local_count):
        enc_cast[pl.ds(a * key_len, key_len), :] = encoded[a].astype(BF16)

    pl.semaphore_wait(
        barrier,
        sections
        - 1
        + others
        + jnp.where(stays, 0, 1)
        + jnp.where(p > 0, 1, 0)
        + jnp.where(p < groups - 1, 1, 0),
    )

    m_rows, m_cols = region(section, core)
    mine_there = region(swap_section, core)

    def swap_copy():
        return remote(
            enc_cast,
            enc_all.at[mine_there[0], mine_there[1]],
            swap_send.at[0],
            swap_recv.at[0],
            (swap_section, swap_p, core),
        )

    @pl.when(stays)
    def _():
        copy = pltpu.make_async_copy(enc_cast, enc_all.at[m_rows, m_cols], self_sem.at[0])
        copy.start()
        copy.wait()

    @pl.when(jnp.logical_not(stays))
    def _():
        swap_copy().start()

    taken = jnp.int32(0)
    slot_dialog = [jnp.int32(0)] * cap
    slot_valid = [jnp.int32(0)] * cap
    slot_length = [jnp.int32(0)] * cap
    for d in range(dialogs):
        mine = (owner[d] == p).astype(jnp.int32)
        table[3 * cap + d] = jnp.where(mine == 1, jnp.minimum(taken, cap), cap)
        for c in range(cap):
            hit = mine * (taken == c).astype(jnp.int32)
            slot_dialog[c] = slot_dialog[c] + hit * d
            slot_valid[c] = slot_valid[c] + hit
            slot_length[c] = slot_length[c] + hit * counts[d]
        taken = taken + mine
    for c in range(cap):
        table[c] = slot_dialog[c]
        table[cap + c] = slot_valid[c]
        table[2 * cap + c] = slot_length[c]

    acc[...] = jnp.zeros_like(acc)
    own_grad[...] = jnp.zeros_like(own_grad)

    @pl.when(jnp.logical_not(stays))
    def _():
        remote(
            enc_cast,
            enc_all.at[m_rows, m_cols],
            swap_send.at[0],
            swap_recv.at[0],
            (swap_section, swap_p, core),
        ).wait_recv()

    def block_copy(s, out_sem, device):
        rows, cols = region(s[0], s[1])
        return remote(
            enc_all.at[rows, cols],
            enc_all.at[rows, cols],
            out_sem,
            enc_recv_sem.at[s[0] * cores + s[1]],
            device,
        )

    def spread(i):
        peer = lax.rem(section + i, sections)
        return block_copy((section, core), enc_send_sem.at[peer], (peer, p, core))

    def pass_on(s, j):
        return block_copy(
            (s, core),
            enc_pass_sem.at[s * others + j - 1],
            (section, p, lax.rem(core + j, cores)),
        )

    @pl.loop(1, sections)
    def _(i):
        spread(i).start()

    for j in range(1, cores):
        pass_on(section, j).start()

    for copy in copies:
        copy.wait()

    @pl.loop(1, sections)
    def _(i):
        s = lax.rem(section + sections - i, sections)
        block_copy((s, core), enc_send_sem.at[s], (s, p, core)).wait_recv()
        for j in range(1, cores):
            pass_on(s, j).start()

    @pl.loop(0, sections)
    def _(i):
        s = lax.rem(section + sections - i, sections)
        for j in range(1, cores):
            m = lax.rem(core + j, cores)
            block_copy((s, m), enc_send_sem.at[s], (section, p, m)).wait_recv()

    def hop(way, r):
        return remote(
            send.at[way, r],
            recv.at[way, r],
            send_sem.at[way, r],
            recv_sem.at[way, r],
            (section, p + 1 if way == 0 else p - 1, core),
        )

    def is_first(way):
        return p == 0 if way == 0 else p == groups - 1

    def is_last(way):
        return p == groups - 1 if way == 0 else p == 0

    def far(way):
        return skew(p if way == 0 else groups - 1 - p)

    def within(r, count):
        return jnp.logical_and(r >= 0, r < count)

    def ahead(way, r, i):
        d = lax.rem(r, subs) * per + i
        delta = owner[d] - p if way == 0 else p - owner[d]
        return jnp.full((key_len, HEAD_DIM), delta, jnp.int32)

    def own_rows(b, kv, i):
        return own_grad[b // subs, kv, table[3 * cap + lax.rem(b, subs) * per + i]].astype(F32)

    def project(h):
        for kv in range(2):
            product = dot(enc_all[...], weights[2 * h + kv], 1, 0).astype(BF16)
            part[pl.ds(h * subs, subs), kv] = product.reshape(subs, per, key_len, HEAD_DIM)

    def attend(h):
        cols = pl.ds(pl.multiple_of(h * HEAD_DIM, HEAD_DIM), HEAD_DIM)
        for c in range(cap):
            d = table[c]
            keep = table[cap + c].astype(F32)
            length = table[2 * cap + c]
            keys = (part[h * subs + d // per, 0, lax.rem(d, per)].astype(F32) * keep).astype(BF16)
            values = (
                part[h * subs + d // per, 1, lax.rem(d, per)].astype(F32) * keep
            ).astype(BF16)
            q = queries[c, :, cols]
            g = (grad_out[c, :, cols].astype(F32) * mask[c]).astype(BF16)
            scores = dot(q, keys, 1, 1) * scale
            ok = lax.broadcasted_iota(jnp.int32, scores.shape, 1) < length
            unnormed = jnp.where(ok, jnp.exp(scores), 0.0)
            attention = unnormed / (jnp.sum(unnormed, axis=1, keepdims=True) + (1.0 - keep))
            probs = attention.astype(BF16)
            attn_out[c, :, cols] = dot(probs, values, 1, 0).astype(BF16)
            own_grad[h, 1, c] = dot(probs, g, 0, 0).astype(BF16)
            grad_probs = dot(g, values, 1, 1)
            grad_scores = (
                attention
                * (grad_probs - jnp.sum(attention * grad_probs, axis=1, keepdims=True))
            ).astype(BF16)
            own_grad[h, 0, c] = (dot(grad_scores, q, 0, 0) * scale).astype(BF16)

    rounds = pieces + lag
    steps = rounds + late

    @pl.loop(0, steps)
    def _(t):
        @pl.when(jnp.logical_and(t < pieces, lax.rem(t, subs) == 0))
        def _():
            project(t // subs)

        for way in range(2):
            r = t - far(way)

            @pl.when(within(r, rounds))
            def _(way=way, r=r):
                fwd, bwd = jnp.minimum(r, pieces - 1), jnp.maximum(r - lag, 0)

                @pl.when(jnp.logical_not(is_first(way)))
                def _():
                    hop(way, r).wait_recv()

                @pl.when(jnp.logical_not(jnp.logical_or(is_first(way), is_last(way))))
                def _(fwd=fwd, bwd=bwd):
                    for kv in range(2):
                        for i in range(per):
                            where_to = ahead(way, r, i)
                            came = recv[way, r, kv, i].astype(F32)
                            send[way, r, kv, i] = jnp.where(
                                where_to > 0,
                                came + part[fwd, kv, i].astype(F32),
                                jnp.where(where_to == 0, own_rows(bwd, kv, i), came),
                            ).astype(BF16)

                    hop(way, r).start()

        whole = t - late

        @pl.when(within(whole, pieces))
        def _():
            @pl.when(p == 0)
            def _():
                part[whole] = (part[whole].astype(F32) + recv[1, whole].astype(F32)).astype(BF16)

            @pl.when(p == groups - 1)
            def _():
                part[whole] = (part[whole].astype(F32) + recv[0, whole].astype(F32)).astype(BF16)

            @pl.when(jnp.logical_and(p > 0, p < groups - 1))
            def _():
                part[whole] = (
                    part[whole].astype(F32)
                    + recv[0, whole].astype(F32)
                    + recv[1, whole].astype(F32)
                ).astype(BF16)

            @pl.when(lax.rem(whole, subs) == subs - 1)
            def _():
                attend(whole // subs)

        for way in range(2):

            @pl.when(jnp.logical_and(is_first(way), t < rounds))
            def _(way=way):
                fwd, bwd = jnp.minimum(t, pieces - 1), jnp.maximum(t - lag, 0)
                for kv in range(2):
                    for i in range(per):
                        send[way, t, kv, i] = jnp.where(
                            ahead(way, t, i) > 0,
                            part[fwd, kv, i].astype(F32),
                            own_rows(bwd, kv, i),
                        ).astype(BF16)
                hop(way, t).start()

        done = t - late - lag

        @pl.when(within(done, pieces))
        def _():
            r = done + lag

            def collect(below, above):
                for kv in range(2):
                    for i in range(per):
                        where_to = ahead(0, r, i)
                        rows = own_rows(done, kv, i)
                        if below:
                            rows = jnp.where(where_to < 0, recv[0, r, kv, i].astype(F32), rows)
                        if above:
                            rows = jnp.where(where_to > 0, recv[1, r, kv, i].astype(F32), rows)
                        part[done, kv, i] = rows.astype(BF16)

            @pl.when(p == 0)
            def _():
                collect(False, True)

            @pl.when(p == groups - 1)
            def _():
                collect(True, False)

            @pl.when(jnp.logical_and(p > 0, p < groups - 1))
            def _():
                collect(True, True)

            @pl.when(lax.rem(done, subs) == subs - 1)
            def _():
                h = done // subs
                for kv in range(2):
                    grads = part[pl.ds(h * subs, subs), kv].reshape(dialogs * key_len, HEAD_DIM)
                    acc[...] += dot(grads, weights[2 * h + kv], 1, 1)

    d_send[...] = acc[...].astype(BF16)

    def pair_copy(s, j):
        m = lax.rem(core + j, cores)
        rows, cols = region(s, m)
        k = s * others + j - 1
        return remote(
            d_send.at[rows, cols], d_pair.at[k], pair_send_sem.at[k], pair_recv_sem.at[k],
            (section, p, m),
        )

    def term_copy(s):
        return remote(
            d_mid.at[s], d_recv.at[section], d_send_sem.at[s], d_recv_sem.at[section],
            (s, p, core),
        )

    @pl.loop(1, sections + 1)
    def _(i):
        for j in range(1, cores):
            pair_copy(lax.rem(section + i, sections), j).start()

    def paired(s):
        rows, cols = region(s, core)
        total = acc[rows, cols]
        for j in range(1, cores):
            pair_copy(s, j).wait_recv()
            total = total + d_pair[s * others + j - 1].astype(F32)
        return total

    @pl.loop(1, sections)
    def _(i):
        s = lax.rem(section + i, sections)
        d_mid[s] = paired(s).astype(BF16)
        term_copy(s).start()

    acc[m_rows, m_cols] = paired(section)

    @pl.loop(1, sections)
    def _(i):
        s = lax.rem(section + sections - i, sections)
        remote(
            d_mid.at[s], d_recv.at[s], d_send_sem.at[s], d_recv_sem.at[s], (s, p, core)
        ).wait_recv()
        acc[m_rows, m_cols] += d_recv[s].astype(F32)

    d_fin[...] = acc[m_rows, m_cols].astype(BF16)

    def back_copy():
        return remote(
            d_fin, d_arrived, swap_send.at[1], swap_recv.at[1], (swap_section, swap_p, core)
        )

    @pl.when(stays)
    def _():
        for a in range(local_count):
            d_encoded[a] = d_fin[pl.ds(a * key_len, key_len), :].astype(F32)

    @pl.when(jnp.logical_not(stays))
    def _():
        back_copy().start()

    @pl.loop(0, rounds)
    def _(r):
        for way in range(2):

            @pl.when(jnp.logical_not(is_last(way)))
            def _(way=way):
                hop(way, r).wait_send()

    @pl.loop(1, sections)
    def _(i):
        spread(i).wait_send()
        term_copy(lax.rem(section + i, sections)).wait_send()

    @pl.loop(0, sections)
    def _(s):
        for j in range(1, cores):
            pass_on(s, j).wait_send()
            pair_copy(s, j).wait_send()

    @pl.when(jnp.logical_not(stays))
    def _():
        swap_copy().wait_send()
        back_copy().wait()
        for a in range(local_count):
            d_encoded[a] = d_arrived[pl.ds(a * key_len, key_len), :].astype(F32)


def body(dims, encoded, counts, owner, w_key, w_value, queries, grad_out, dec_mask):
    sections, groups, cores = dims
    local_count, key_len, feat = encoded.shape
    dialogs = local_count * groups
    cap, query_len, width = queries.shape[1:]
    model_rows = w_key.shape[1]
    heads = width // HEAD_DIM
    per = local_count
    pieces = heads * groups
    rounds = pieces + lag_of(groups)
    others = cores - 1
    block_rows = local_count * key_len
    item = (2, per, key_len, HEAD_DIM)
    dma = pltpu.SemaphoreType.DMA
    vmem = pl.BlockSpec(memory_space=pltpu.VMEM)
    smem = pl.BlockSpec(memory_space=pltpu.SMEM)
    hbm = pl.BlockSpec(memory_space=pl.ANY)
    mask = dec_mask.astype(F32)[:, :, None]
    attended, d_encoded = pl.pallas_call(
        functools.partial(kernel, dims),
        out_shape=(
            jax.ShapeDtypeStruct((cap, query_len, width), BF16),
            jax.ShapeDtypeStruct((local_count, key_len, feat), F32),
        ),
        in_specs=[smem, smem, vmem, hbm, hbm, vmem, vmem, vmem],
        out_specs=(vmem, vmem),
        scratch_shapes=[
            pltpu.SMEM((3 * cap + dialogs,), jnp.int32),
            pltpu.VMEM((2 * heads, model_rows, HEAD_DIM), BF16),
            pltpu.VMEM((block_rows, feat), BF16),
            pltpu.VMEM((dialogs * key_len, model_rows), BF16),
            pltpu.VMEM((pieces,) + item, BF16),
            pltpu.VMEM((2, rounds) + item, BF16),
            pltpu.VMEM((2, rounds) + item, BF16),
            pltpu.VMEM((heads, 2, cap + 1, key_len, HEAD_DIM), BF16),
            pltpu.VMEM((dialogs * key_len, model_rows), F32),
            pltpu.VMEM((dialogs * key_len, model_rows), BF16),
            pltpu.VMEM((sections * others, block_rows, feat), BF16),
            pltpu.VMEM((sections, block_rows, feat), BF16),
            pltpu.VMEM((sections, block_rows, feat), BF16),
            pltpu.VMEM((block_rows, feat), BF16),
            pltpu.VMEM((block_rows, feat), BF16),
            dma((2 * heads,)),
            dma((2,)),
            dma((2,)),
            dma((1,)),
            dma((sections,)),
            dma((sections * others,)),
            dma((sections * cores,)),
            dma((2, rounds)),
            dma((2, rounds)),
            dma((sections * others,)),
            dma((sections * others,)),
            dma((sections,)),
            dma((sections,)),
        ],
        compiler_params=pltpu.CompilerParams(
            collective_id=0, has_side_effects=True, vmem_limit_bytes=60 * 1024 * 1024
        ),
    )(counts, owner, encoded, w_key[0], w_value[0], queries[0], grad_out[0], mask)
    return (attended[None], d_encoded)


def solution(mesh):
    placed = (
        P("dp", None, ("section", "mp")),
        P(),
        P(),
        P("section", "dp", "mp"),
        P("section", "dp", "mp"),
        P("section", "dp", None, "mp"),
        P("section", "dp", None, "mp"),
        P("dp", None),
    )
    dims = tuple(mesh.shape[name] for name in ("section", "dp", "mp"))
    return jax.shard_map(
        functools.partial(body, dims),
        mesh=mesh,
        in_specs=placed,
        out_specs=(P("section", "dp", None, "mp"), P("dp", None, ("section", "mp"))),
        check_vma=False,
    )
```

profile of v0, /device:TPU:25, one launch (start us, length us, event | category | flops | bytes accessed | tf_op | source)
XLA Modules:
  0.0 140.5 jit_solution(2055923801177537904)
XLA Ops:
  0.6 0.7 convert_bitcast_fusion
  1.3 0.9 copy.10.mask
  2.2 135.3 %shard_map.95 = (bf16[4,128,1024]{2,1,0:T(8,128)(2,1)}, f32[2,64,512]{2,1,0:T(8,128)}) custom-call(s32[8]{0:T(128)} %counts.1, s32[8]{0:T(128)} %owner.1, f32[2,64,512]{2,1,0:T(8,128)} %encoded.1, bf16[1024,1024]{1,0:T(8,128)(2,1)} %bitcast.7, bf16[1024,1024]{1,0:T(8,128)(2,1)} %bitcast.8, bf16[4,128,1024]{2,1,0:T(8,128)(2,1)} %bitcast.10, ...), custom_call_target="tpu_custom_call" | custom-call | tf_op jit(solution)/shard_map/pallas_call | solution.py:528
  137.5 0.0 copy-start
  137.5 2.3 %copy.13 = bf16[1,4,128,1024]{3,2,1,0:T(8,128)(2,1)} copy(bf16[1,4,128,1024]{3,2,1,0:T(8,128)(2,1)} %bitcast.9) | data formatting | bytes 2097152
  139.8 0.0 copy-done
  139.8 0.7 copy.14
Async XLA Ops:
  137.5 2.3 %copy-start = (f32[2,64,512]{2,1,0:T(8,128)S(1)}, f32[2,64,512]{2,1,0:T(8,128)}, u32[]{:S(2)}) copy-start(f32[2,64,512]{2,1,0:T(8,128)} %get-tuple-element.9) | copy-start | bytes 786436
where the time goes:
time: 141 us
  Pallas kernels  135 us (96%)
  local copies, waits for them, and re-layouts  3.87 us (3%)
    pallas_call x1, Pallas kernels, body(): pl.pallas_call(functools.partial(kernel, dims), out_shape=(jax.ShapeDtype...  135 us
    unnamed x4, local copies, waits for them, and re-layouts  3.01 us

commit v1 on v0

--- a/solution.py
+++ b/solution.py
@@ -13,12 +13,19 @@
 BF16 = jnp.bfloat16
 
 
+PIECE_ROWS = 64
+
+
 def skew(hops):
-    return (5 * hops + 2) // 3
-
-
-def lag_of(groups):
-    return pl.cdiv(groups - 1 + skew(groups - 1), groups) * groups
+    return (5 * hops + 1) // 2
+
+
+def packed_rows(dialogs, key_len):
+    return dialogs * key_len * 3 // 4
+
+
+def lag_of(subs, groups):
+    return subs - 1 + skew(groups - 1)
 
 
 def dot(left, right, left_dim, right_dim):
@@ -41,13 +48,24 @@
     d_encoded,
     table,
     weights,
+    q_buf,
+    g_buf,
+    out_buf,
     enc_cast,
     enc_all,
+    enc_pack,
+    to_packed,
+    from_packed,
+    take_slots,
+    give_slots,
+    delta,
     part,
     recv,
     send,
-    own_grad,
+    own,
+    slot_grad,
     acc,
+    fin,
     d_send,
     d_pair,
     d_mid,
@@ -55,6 +73,8 @@
     d_fin,
     d_arrived,
     w_sem,
+    io_sem,
+    out_sem,
     swap_send,
     swap_recv,
     self_sem,
@@ -78,10 +98,11 @@
     block_rows = local_count * key_len
     cap = queries.shape[0]
     heads = queries.shape[2] // HEAD_DIM
-    per = local_count
-    subs = groups
+    packed = packed_rows(dialogs, key_len)
+    piece_rows = min(PIECE_ROWS, packed)
+    subs = packed // piece_rows
     pieces = heads * subs
-    lag = lag_of(groups)
+    lag = lag_of(subs, groups)
     late = skew(groups - 1)
     others = cores - 1
     scale = HEAD_DIM ** (-0.5)
@@ -139,6 +160,11 @@
             copy.start()
             copies.append(copy)
 
+    for k, (ref, buf) in enumerate(((queries, q_buf), (grad_out, g_buf))):
+        copy = pltpu.make_async_copy(ref, buf, io_sem.at[k])
+        copy.start()
+        copies.append(copy)
+
     for a in range(local_count):
         enc_cast[pl.ds(a * key_len, key_len), :] = encoded[a].astype(BF16)
 
@@ -175,25 +201,60 @@
         swap_copy().start()
 
     taken = jnp.int32(0)
-    slot_dialog = [jnp.int32(0)] * cap
+    start = jnp.int32(0)
+    starts = []
+    slot_start = [jnp.int32(0)] * cap
     slot_valid = [jnp.int32(0)] * cap
     slot_length = [jnp.int32(0)] * cap
     for d in range(dialogs):
         mine = (owner[d] == p).astype(jnp.int32)
-        table[3 * cap + d] = jnp.where(mine == 1, jnp.minimum(taken, cap), cap)
         for c in range(cap):
             hit = mine * (taken == c).astype(jnp.int32)
-            slot_dialog[c] = slot_dialog[c] + hit * d
+            slot_start[c] = slot_start[c] + hit * start
             slot_valid[c] = slot_valid[c] + hit
             slot_length[c] = slot_length[c] + hit * counts[d]
         taken = taken + mine
+        starts.append(start)
+        start = start + counts[d]
     for c in range(cap):
-        table[c] = slot_dialog[c]
-        table[cap + c] = slot_valid[c]
-        table[2 * cap + c] = slot_length[c]
+        table[c] = slot_valid[c]
+        table[cap + c] = slot_length[c]
+
+    def one_hot(hit):
+        return jnp.where(hit, 1.0, 0.0).astype(BF16)
+
+    def spread_rows(out, firsts, lengths):
+        shape = (packed, len(firsts) * key_len)
+        at = lax.broadcasted_iota(jnp.int32, (1, shape[1]), 1)
+        place = jnp.full((1, shape[1]), -1, jnp.int32)
+        for k, (first, length) in enumerate(zip(firsts, lengths)):
+            inside = jnp.logical_and(at >= k * key_len, at < k * key_len + length)
+            place = jnp.where(inside, at - k * key_len + first, place)
+        out[...] = one_hot(lax.broadcasted_iota(jnp.int32, shape, 0) == place)
+
+    def take_rows(out, firsts, lengths):
+        shape = (key_len, packed)
+        row = lax.broadcasted_iota(jnp.int32, shape, 0)
+        col = lax.broadcasted_iota(jnp.int32, shape, 1)
+        for k, (first, length) in enumerate(zip(firsts, lengths)):
+            hit = jnp.logical_and(col == row + first, row < length)
+            out[pl.ds(k * key_len, key_len), :] = one_hot(hit)
+
+    lengths = [counts[d] for d in range(dialogs)]
+    spread_rows(to_packed, starts, lengths)
+    take_rows(from_packed, starts, lengths)
+    take_rows(take_slots, slot_start, slot_length)
+    spread_rows(give_slots, slot_start, slot_length)
+
+    for b in range(subs):
+        row = lax.broadcasted_iota(jnp.int32, (piece_rows, HEAD_DIM), 0) + b * piece_rows
+        ahead_by = jnp.full((piece_rows, HEAD_DIM), groups, jnp.int32)
+        for d in range(dialogs):
+            ahead_by = jnp.where(row >= starts[d], owner[d] - p, ahead_by)
+        delta[b] = ahead_by
 
     acc[...] = jnp.zeros_like(acc)
-    own_grad[...] = jnp.zeros_like(own_grad)
+    own[...] = jnp.zeros_like(own)
 
     @pl.when(jnp.logical_not(stays))
     def _():
@@ -271,44 +332,63 @@
     def within(r, count):
         return jnp.logical_and(r >= 0, r < count)
 
-    def ahead(way, r, i):
-        d = lax.rem(r, subs) * per + i
-        delta = owner[d] - p if way == 0 else p - owner[d]
-        return jnp.full((key_len, HEAD_DIM), delta, jnp.int32)
-
-    def own_rows(b, kv, i):
-        return own_grad[b // subs, kv, table[3 * cap + lax.rem(b, subs) * per + i]].astype(F32)
+    def ahead(way, r):
+        by = delta[lax.rem(r, subs)]
+        return by if way == 0 else -by
+
+    def back_piece(r):
+        q = jnp.maximum(r - lag, 0)
+        return (q // subs) * subs + lax.rem(r, subs)
+
+    enc_pack[...] = dot(to_packed[...], enc_all[...], 1, 0).astype(BF16)
 
     def project(h):
         for kv in range(2):
-            product = dot(enc_all[...], weights[2 * h + kv], 1, 0).astype(BF16)
-            part[pl.ds(h * subs, subs), kv] = product.reshape(subs, per, key_len, HEAD_DIM)
+            product = dot(enc_pack[...], weights[2 * h + kv], 1, 0).astype(BF16)
+            part[pl.ds(h * subs, subs), kv] = product.reshape(subs, piece_rows, HEAD_DIM)
+
+    def out_copy(h):
+        cols = pl.ds(pl.multiple_of(h * HEAD_DIM, HEAD_DIM), HEAD_DIM)
+        return pltpu.make_async_copy(out_buf.at[h], attn_out.at[:, :, cols], out_sem.at[h])
 
     def attend(h):
         cols = pl.ds(pl.multiple_of(h * HEAD_DIM, HEAD_DIM), HEAD_DIM)
+        mine = [
+            dot(
+                take_slots[...],
+                part[pl.ds(h * subs, subs), kv].reshape(packed, HEAD_DIM),
+                1,
+                0,
+            ).astype(BF16)
+            for kv in range(2)
+        ]
         for c in range(cap):
-            d = table[c]
-            keep = table[cap + c].astype(F32)
-            length = table[2 * cap + c]
-            keys = (part[h * subs + d // per, 0, lax.rem(d, per)].astype(F32) * keep).astype(BF16)
-            values = (
-                part[h * subs + d // per, 1, lax.rem(d, per)].astype(F32) * keep
-            ).astype(BF16)
-            q = queries[c, :, cols]
-            g = (grad_out[c, :, cols].astype(F32) * mask[c]).astype(BF16)
-            scores = dot(q, keys, 1, 1) * scale
-            ok = lax.broadcasted_iota(jnp.int32, scores.shape, 1) < length
+            keep = table[c].astype(F32)
+            length = table[cap + c]
+            keys = mine[0][c * key_len : (c + 1) * key_len]
+            values = mine[1][c * key_len : (c + 1) * key_len]
+            q = q_buf[c, :, cols]
+            g = g_buf[c, :, cols]
+            live = mask[pl.ds(c, 1), :].astype(F32)
+            scores = dot(keys, q, 1, 1) * scale
+            ok = lax.broadcasted_iota(jnp.int32, scores.shape, 0) < length
             unnormed = jnp.where(ok, jnp.exp(scores), 0.0)
-            attention = unnormed / (jnp.sum(unnormed, axis=1, keepdims=True) + (1.0 - keep))
+            attention = unnormed / (jnp.sum(unnormed, axis=0, keepdims=True) + (1.0 - keep))
             probs = attention.astype(BF16)
-            attn_out[c, :, cols] = dot(probs, values, 1, 0).astype(BF16)
-            own_grad[h, 1, c] = dot(probs, g, 0, 0).astype(BF16)
-            grad_probs = dot(g, values, 1, 1)
+            out_buf[h, c] = dot(probs, values, 0, 0).astype(BF16)
+            grad_probs = dot(values, g, 1, 1) * live
+            live_probs = (probs.astype(F32) * live).astype(BF16)
+            rows = pl.ds(c * key_len, key_len)
+            slot_grad[1, rows, :] = dot(live_probs, g, 1, 0).astype(BF16)
             grad_scores = (
                 attention
-                * (grad_probs - jnp.sum(attention * grad_probs, axis=1, keepdims=True))
+                * (grad_probs - jnp.sum(attention * grad_probs, axis=0, keepdims=True))
             ).astype(BF16)
-            own_grad[h, 0, c] = (dot(grad_scores, q, 0, 0) * scale).astype(BF16)
+            slot_grad[0, rows, :] = (dot(grad_scores, q, 1, 0) * scale).astype(BF16)
+        for kv in range(2):
+            mine_rows = dot(give_slots[...], slot_grad[kv], 1, 0).astype(BF16)
+            own[pl.ds(h * subs, subs), kv] = mine_rows.reshape(subs, piece_rows, HEAD_DIM)
+        out_copy(h).start()
 
     rounds = pieces + lag
     steps = rounds + late
@@ -324,7 +404,7 @@
 
             @pl.when(within(r, rounds))
             def _(way=way, r=r):
-                fwd, bwd = jnp.minimum(r, pieces - 1), jnp.maximum(r - lag, 0)
+                fwd, bwd = jnp.minimum(r, pieces - 1), back_piece(r)
 
                 @pl.when(jnp.logical_not(is_first(way)))
                 def _():
@@ -332,15 +412,14 @@
 
                 @pl.when(jnp.logical_not(jnp.logical_or(is_first(way), is_last(way))))
                 def _(fwd=fwd, bwd=bwd):
+                    where_to = ahead(way, r)
                     for kv in range(2):
-                        for i in range(per):
-                            where_to = ahead(way, r, i)
-                            came = recv[way, r, kv, i].astype(F32)
-                            send[way, r, kv, i] = jnp.where(
-                                where_to > 0,
-                                came + part[fwd, kv, i].astype(F32),
-                                jnp.where(where_to == 0, own_rows(bwd, kv, i), came),
-                            ).astype(BF16)
+                        came = recv[way, r, kv].astype(F32)
+                        send[way, r, kv] = jnp.where(
+                            where_to > 0,
+                            came + part[fwd, kv].astype(F32),
+                            jnp.where(where_to == 0, own[bwd, kv].astype(F32), came),
+                        ).astype(BF16)
 
                     hop(way, r).start()
 
@@ -372,14 +451,12 @@
 
             @pl.when(jnp.logical_and(is_first(way), t < rounds))
             def _(way=way):
-                fwd, bwd = jnp.minimum(t, pieces - 1), jnp.maximum(t - lag, 0)
+                fwd, bwd = jnp.minimum(t, pieces - 1), back_piece(t)
+                where_to = ahead(way, t)
                 for kv in range(2):
-                    for i in range(per):
-                        send[way, t, kv, i] = jnp.where(
-                            ahead(way, t, i) > 0,
-                            part[fwd, kv, i].astype(F32),
-                            own_rows(bwd, kv, i),
-                        ).astype(BF16)
+                    send[way, t, kv] = jnp.where(
+                        where_to > 0, part[fwd, kv].astype(F32), own[bwd, kv].astype(F32)
+                    ).astype(BF16)
                 hop(way, t).start()
 
         done = t - late - lag
@@ -387,17 +464,17 @@
         @pl.when(within(done, pieces))
         def _():
             r = done + lag
+            back = back_piece(r)
 
             def collect(below, above):
+                where_to = ahead(0, r)
                 for kv in range(2):
-                    for i in range(per):
-                        where_to = ahead(0, r, i)
-                        rows = own_rows(done, kv, i)
-                        if below:
-                            rows = jnp.where(where_to < 0, recv[0, r, kv, i].astype(F32), rows)
-                        if above:
-                            rows = jnp.where(where_to > 0, recv[1, r, kv, i].astype(F32), rows)
-                        part[done, kv, i] = rows.astype(BF16)
+                    rows = own[back, kv].astype(F32)
+                    if below:
+                        rows = jnp.where(where_to < 0, recv[0, r, kv].astype(F32), rows)
+                    if above:
+                        rows = jnp.where(where_to > 0, recv[1, r, kv].astype(F32), rows)
+                    part[back, kv] = rows.astype(BF16)
 
             @pl.when(p == 0)
             def _():
@@ -414,11 +491,14 @@
             @pl.when(lax.rem(done, subs) == subs - 1)
             def _():
                 h = done // subs
-                for kv in range(2):
-                    grads = part[pl.ds(h * subs, subs), kv].reshape(dialogs * key_len, HEAD_DIM)
-                    acc[...] += dot(grads, weights[2 * h + kv], 1, 1)
-
-    d_send[...] = acc[...].astype(BF16)
+                grads = [
+                    part[pl.ds(h * subs, subs), kv].reshape(packed, HEAD_DIM) for kv in range(2)
+                ]
+                acc[...] += dot(grads[0], weights[2 * h], 1, 1) + dot(
+                    grads[1], weights[2 * h + 1], 1, 1
+                )
+
+    d_send[...] = dot(from_packed[...], acc[...].astype(BF16), 1, 0).astype(BF16)
 
     def pair_copy(s, j):
         m = lax.rem(core + j, cores)
@@ -442,7 +522,7 @@
 
     def paired(s):
         rows, cols = region(s, core)
-        total = acc[rows, cols]
+        total = d_send[rows, cols].astype(F32)
         for j in range(1, cores):
             pair_copy(s, j).wait_recv()
             total = total + d_pair[s * others + j - 1].astype(F32)
@@ -454,7 +534,7 @@
         d_mid[s] = paired(s).astype(BF16)
         term_copy(s).start()
 
-    acc[m_rows, m_cols] = paired(section)
+    fin[...] = paired(section)
 
     @pl.loop(1, sections)
     def _(i):
@@ -462,9 +542,9 @@
         remote(
             d_mid.at[s], d_recv.at[s], d_send_sem.at[s], d_recv_sem.at[s], (s, p, core)
         ).wait_recv()
-        acc[m_rows, m_cols] += d_recv[s].astype(F32)
-
-    d_fin[...] = acc[m_rows, m_cols].astype(BF16)
+        fin[...] += d_recv[s].astype(F32)
+
+    d_fin[...] = fin[...].astype(BF16)
 
     def back_copy():
         return remote(
@@ -479,6 +559,9 @@
     @pl.when(jnp.logical_not(stays))
     def _():
         back_copy().start()
+
+    for h in range(heads):
+        out_copy(h).wait()
 
     @pl.loop(0, rounds)
     def _(r):
@@ -514,35 +597,48 @@
     cap, query_len, width = queries.shape[1:]
     model_rows = w_key.shape[1]
     heads = width // HEAD_DIM
-    per = local_count
-    pieces = heads * groups
-    rounds = pieces + lag_of(groups)
+    packed = packed_rows(dialogs, key_len)
+    piece_rows = min(PIECE_ROWS, packed)
+    subs = packed // piece_rows
+    pieces = heads * subs
+    rounds = pieces + lag_of(subs, groups)
     others = cores - 1
     block_rows = local_count * key_len
-    item = (2, per, key_len, HEAD_DIM)
+    item = (2, piece_rows, HEAD_DIM)
+    rows = dialogs * key_len
     dma = pltpu.SemaphoreType.DMA
     vmem = pl.BlockSpec(memory_space=pltpu.VMEM)
     smem = pl.BlockSpec(memory_space=pltpu.SMEM)
     hbm = pl.BlockSpec(memory_space=pl.ANY)
-    mask = dec_mask.astype(F32)[:, :, None]
     attended, d_encoded = pl.pallas_call(
         functools.partial(kernel, dims),
         out_shape=(
             jax.ShapeDtypeStruct((cap, query_len, width), BF16),
             jax.ShapeDtypeStruct((local_count, key_len, feat), F32),
         ),
-        in_specs=[smem, smem, vmem, hbm, hbm, vmem, vmem, vmem],
-        out_specs=(vmem, vmem),
+        in_specs=[smem, smem, vmem, hbm, hbm, hbm, hbm, vmem],
+        out_specs=(hbm, vmem),
         scratch_shapes=[
-            pltpu.SMEM((3 * cap + dialogs,), jnp.int32),
+            pltpu.SMEM((2 * cap,), jnp.int32),
             pltpu.VMEM((2 * heads, model_rows, HEAD_DIM), BF16),
+            pltpu.VMEM((cap, query_len, width), BF16),
+            pltpu.VMEM((cap, query_len, width), BF16),
+            pltpu.VMEM((heads, cap, query_len, HEAD_DIM), BF16),
             pltpu.VMEM((block_rows, feat), BF16),
-            pltpu.VMEM((dialogs * key_len, model_rows), BF16),
+            pltpu.VMEM((rows, model_rows), BF16),
+            pltpu.VMEM((packed, model_rows), BF16),
+            pltpu.VMEM((packed, rows), BF16),
+            pltpu.VMEM((rows, packed), BF16),
+            pltpu.VMEM((cap * key_len, packed), BF16),
+            pltpu.VMEM((packed, cap * key_len), BF16),
+            pltpu.VMEM((subs, piece_rows, HEAD_DIM), jnp.int32),
             pltpu.VMEM((pieces,) + item, BF16),
             pltpu.VMEM((2, rounds) + item, BF16),
             pltpu.VMEM((2, rounds) + item, BF16),
-            pltpu.VMEM((heads, 2, cap + 1, key_len, HEAD_DIM), BF16),
-            pltpu.VMEM((dialogs * key_len, model_rows), F32),
+            pltpu.VMEM((pieces,) + item, BF16),
+            pltpu.VMEM((2, cap * key_len, HEAD_DIM), BF16),
+            pltpu.VMEM((packed, model_rows), F32),
+            pltpu.VMEM((block_rows, feat), F32),
             pltpu.VMEM((dialogs * key_len, model_rows), BF16),
             pltpu.VMEM((sections * others, block_rows, feat), BF16),
             pltpu.VMEM((sections, block_rows, feat), BF16),
@@ -550,6 +646,8 @@
             pltpu.VMEM((block_rows, feat), BF16),
             pltpu.VMEM((block_rows, feat), BF16),
             dma((2 * heads,)),
+            dma((2,)),
+            dma((heads,)),
             dma((2,)),
             dma((2,)),
             dma((1,)),
@@ -566,7 +664,7 @@
         compiler_params=pltpu.CompilerParams(
             collective_id=0, has_side_effects=True, vmem_limit_bytes=60 * 1024 * 1024
         ),
-    )(counts, owner, encoded, w_key[0], w_value[0], queries[0], grad_out[0], mask)
+    )(counts, owner, encoded, w_key[0], w_value[0], queries[0], grad_out[0], dec_mask)
     return (attended[None], d_encoded)
 
 

time: 141 us -> 118 us (0.84)
  the two profiles are of different devices: /device:TPU:25 before, /device:TPU:3 now
where the time goes in v1:
time: 118 us; the launch traced here: 117 us
  Pallas kernels  114 us (97%)
  local copies, waits for them, and re-layouts  3.01 us (3%)
    pallas_call x1, Pallas kernels, body(): pl.pallas_call(functools.partial(kernel, dims), out_shape=(jax.ShapeDtype...  114 us
    unnamed x4, local copies, waits for them, and re-layouts  3.01 us

profile of v1, /device:TPU:3, one launch (start us, length us, event | category | flops | bytes accessed | tf_op | source)
XLA Modules:
  0.0 117.3 jit_solution(8351595462670849695)
XLA Ops:
  0.6 113.7 %shard_map.95 = (bf16[4,128,1024]{2,1,0:T(8,128)(2,1)}, f32[2,64,512]{2,1,0:T(8,128)}) custom-call(s32[8]{0:T(128)} %counts.1, s32[8]{0:T(128)} %owner.1, f32[2,64,512]{2,1,0:T(8,128)} %encoded.1, bf16[1024,1024]{1,0:T(8,128)(2,1)} %bitcast.5, bf16[1024,1024]{1,0:T(8,128)(2,1)} %bitcast.6, bf16[4,128,1024]{2,1,0:T(8,128)(2,1)} %bitcast.7, ...), custom_call_target="tpu_custom_call" | custom-call | tf_op jit(solution)/shard_map/pallas_call | solution.py:613
  114.3 0.0 copy-start
  114.3 2.3 %copy.12 = bf16[1,4,128,1024]{3,2,1,0:T(8,128)(2,1)} copy(bf16[1,4,128,1024]{3,2,1,0:T(8,128)(2,1)} %bitcast.9) | data formatting | bytes 2097152
  116.6 0.0 copy-done
  116.6 0.7 copy.13
Async XLA Ops:
  114.3 2.3 %copy-start = (f32[2,64,512]{2,1,0:T(8,128)S(1)}, f32[2,64,512]{2,1,0:T(8,128)}, u32[]{:S(2)}) copy-start(f32[2,64,512]{2,1,0:T(8,128)} %get-tuple-element.9) | copy-start | bytes 786436

commit v2 on v1

v2 whole, which is shorter than its diff:
```python
import functools

import jax
import jax.numpy as jnp
from jax import lax
from jax.experimental import pallas as pl
from jax.experimental.pallas import tpu as pltpu
from jax.sharding import PartitionSpec as P

HEAD_DIM = 256
MESH = pl.DeviceIdType.MESH
F32 = jnp.float32
BF16 = jnp.bfloat16


PIECE_ROWS = 128
TOP = 0


def skew(hops):
    return 3 * hops


def packed_rows(dialogs, key_len):
    return dialogs * key_len * 3 // 4


def lag_of(subs, groups):
    return subs - 1 + TOP + skew(groups - 1)


def dot(left, right, left_dim, right_dim):
    return lax.dot_general(
        left, right, (((left_dim,), (right_dim,)), ((), ())), preferred_element_type=F32
    )


def kernel(
    dims,
    counts,
    owner,
    encoded,
    w_key,
    w_value,
    queries,
    grad_out,
    mask,
    attn_out,
    d_encoded,
    table,
    weights,
    q_buf,
    g_buf,
    out_buf,
    enc_cast,
    enc_all,
    enc_pack,
    to_packed,
    from_packed,
    take_slots,
    give_slots,
    delta,
    part,
    recv,
    send,
    own,
    slot_grad,
    held,
    acc,
    d_send,
    d_pair,
    d_mid,
    d_recv,
    d_fin,
    d_cross,
    d_out,
    mid,
    w_sem,
    io_sem,
    out_sem,
    scatter_send,
    scatter_recv,
    along_send,
    along_recv,
    fan_send,
    pass_send,
    block_recv,
    send_sem,
    recv_sem,
    pair_send,
    pair_recv,
    term_send,
    term_recv,
    cross_send,
    cross_recv,
    last_send,
    last_recv,
):
    sections, groups, cores = dims
    section = lax.axis_index("section")
    p = lax.axis_index("dp")
    core = lax.axis_index("mp")
    fold = sections // groups
    local_count, key_len, feat = encoded.shape
    dialogs = local_count * groups
    block_rows = local_count * key_len
    cap = queries.shape[0]
    heads = queries.shape[2] // HEAD_DIM
    packed = packed_rows(dialogs, key_len)
    piece_rows = min(PIECE_ROWS, packed)
    subs = packed // piece_rows
    halves = 2 * heads
    pieces = halves * subs
    lag = lag_of(subs, groups)
    late = skew(groups - 1)
    others = cores - 1
    scale = HEAD_DIM ** (-0.5)

    chunk = block_rows // sections
    spans = [divmod(j * chunk, key_len) for j in range(sections)]

    def remote(src, dst, out_sem, in_sem, device):
        return pltpu.make_async_remote_copy(
            src_ref=src,
            dst_ref=dst,
            send_sem=out_sem,
            recv_sem=in_sem,
            device_id=device,
            device_id_type=MESH,
        )

    barrier = pltpu.get_barrier_semaphore()

    def greet(s, z, m):
        pl.semaphore_signal(barrier, inc=1, device_id=(s, z, m), device_id_type=MESH)

    @pl.loop(1, groups)
    def _(i):
        greet(section, lax.rem(p + i, groups), core)

    @pl.loop(1, sections)
    def _(i):
        greet(lax.rem(section + i, sections), p, core)

    for j in range(1, cores):
        greet(section, p, lax.rem(core + j, cores))

    copies = []
    for h in range(heads):
        for kv, ref in enumerate((w_key, w_value)):
            copy = pltpu.make_async_copy(
                ref.at[:, pl.ds(h * HEAD_DIM, HEAD_DIM)],
                weights.at[2 * h + kv],
                w_sem.at[2 * h + kv],
            )
            copy.start()
            copies.append(copy)

    for k, (ref, buf) in enumerate(((queries, q_buf), (grad_out, g_buf))):
        copy = pltpu.make_async_copy(ref, buf, io_sem.at[k])
        copy.start()
        copies.append(copy)

    for j, (a, first) in enumerate(spans):
        enc_cast[j] = encoded[a, pl.ds(first, chunk), :].astype(BF16)
    mid[section] = enc_cast[section]

    pl.semaphore_wait(barrier, sections - 1 + groups - 1 + others)

    def scatter(s, to):
        return remote(
            enc_cast.at[to], mid.at[s], scatter_send.at[to], scatter_recv.at[s], (to, p, core)
        )

    @pl.loop(1, sections)
    def _(i):
        scatter(section, lax.rem(section + i, sections)).start()

    def near(k):
        return lax.rem(p + k * jnp.where(2 * p < groups, 1, groups - 1), groups)

    def along(z, f, s):
        return remote(
            mid.at[s],
            enc_all.at[f * cores + core, z, section],
            along_send.at[s],
            along_recv.at[z * fold + f],
            (section, s // fold, core),
        )

    @pl.loop(0, sections)
    def _(i):
        s = lax.rem(section + i, sections)

        @pl.when(i > 0)
        def _():
            scatter(s, s).wait_recv()

        @pl.when(s // fold == p)
        def _():
            enc_all[lax.rem(s, fold) * cores + core, p, section] = mid[s]

        @pl.when(s // fold != p)
        def _():
            along(p, lax.rem(s, fold), s).start()

    taken = jnp.int32(0)
    start = jnp.int32(0)
    starts = []
    slot_start = [jnp.int32(0)] * cap
    slot_valid = [jnp.int32(0)] * cap
    slot_length = [jnp.int32(0)] * cap
    for d in range(dialogs):
        mine = (owner[d] == p).astype(jnp.int32)
        for c in range(cap):
            hit = mine * (taken == c).astype(jnp.int32)
            slot_start[c] = slot_start[c] + hit * start
            slot_valid[c] = slot_valid[c] + hit
            slot_length[c] = slot_length[c] + hit * counts[d]
        taken = taken + mine
        starts.append(start)
        start = start + counts[d]
    for c in range(cap):
        table[c] = slot_valid[c]
        table[cap + c] = slot_length[c]

    def one_hot(hit):
        return jnp.where(hit, 1.0, 0.0).astype(BF16)

    def spread_rows(out, firsts, lengths):
        shape = (packed, len(firsts) * key_len)
        at = lax.broadcasted_iota(jnp.int32, (1, shape[1]), 1)
        place = jnp.full((1, shape[1]), -1, jnp.int32)
        for k, (first, length) in enumerate(zip(firsts, lengths)):
            inside = jnp.logical_and(at >= k * key_len, at < k * key_len + length)
            place = jnp.where(inside, at - k * key_len + first, place)
        out[...] = one_hot(lax.broadcasted_iota(jnp.int32, shape, 0) == place)

    def take_rows(out, firsts, lengths):
        shape = (key_len, packed)
        row = lax.broadcasted_iota(jnp.int32, shape, 0)
        col = lax.broadcasted_iota(jnp.int32, shape, 1)
        for k, (first, length) in enumerate(zip(firsts, lengths)):
            hit = jnp.logical_and(col == row + first, row < length)
            out[pl.ds(k * key_len, key_len), :] = one_hot(hit)

    lengths = [counts[d] for d in range(dialogs)]
    spread_rows(to_packed, starts, lengths)
    take_rows(from_packed, starts, lengths)
    take_rows(take_slots, slot_start, slot_length)
    spread_rows(give_slots, slot_start, slot_length)

    for b in range(subs):
        row = lax.broadcasted_iota(jnp.int32, (piece_rows, HEAD_DIM), 0) + b * piece_rows
        ahead_by = jnp.full((piece_rows, HEAD_DIM), groups, jnp.int32)
        for d in range(dialogs):
            ahead_by = jnp.where(row >= starts[d], owner[d] - p, ahead_by)
        delta[b] = ahead_by

    acc[...] = jnp.zeros_like(acc)
    own[...] = jnp.zeros_like(own)

    def block(j, z, f, m, out_sem, device):
        where = enc_all.at[f * cores + m, z, j]
        in_sem = block_recv.at[(j * sections + z * fold + f) * cores + m]
        return remote(where, where, out_sem, in_sem, device)

    def fan(z, f, to):
        out_sem = fan_send.at[to * sections + z * fold + f]
        return block(section, z, f, core, out_sem, (to, p, core))

    def pass_on(j, z, f, i):
        out_sem = pass_send.at[(j * sections + z * fold + f) * others + i - 1]
        return block(j, z, f, core, out_sem, (section, p, lax.rem(core + i, cores)))

    @pl.loop(0, groups + 1)
    def _(k):
        @pl.when(k < groups)
        def _():
            z = near(k)
            for f in range(fold):

                @pl.when(k > 0)
                def _(f=f):
                    along(z, f, z * fold + f).wait_recv()

                @pl.loop(1, sections)
                def _(i, f=f):
                    fan(z, f, lax.rem(section + i, sections)).start()

                for i in range(1, cores):
                    pass_on(section, z, f, i).start()

        @pl.when(k > 0)
        def _():
            z = near(k - 1)

            @pl.loop(1, sections)
            def _(i):
                j = lax.rem(section + sections - i, sections)
                for f in range(fold):
                    block(j, z, f, core, fan_send.at[0], (j, p, core)).wait_recv()
                    for i in range(1, cores):
                        pass_on(j, z, f, i).start()

    for copy in copies:
        copy.wait()

    @pl.loop(0, sections)
    def _(j):
        @pl.loop(0, groups)
        def _(z):
            for f in range(fold):
                for i in range(1, cores):
                    m = lax.rem(core + i, cores)
                    block(j, z, f, m, fan_send.at[0], (section, p, m)).wait_recv()

    def hop(way, r):
        return remote(
            send.at[way, r],
            recv.at[way, r],
            send_sem.at[way, r],
            recv_sem.at[way, r],
            (section, p + 1 if way == 0 else p - 1, core),
        )

    def is_first(way):
        return p == 0 if way == 0 else p == groups - 1

    def is_last(way):
        return p == groups - 1 if way == 0 else p == 0

    def far(way):
        return skew(p if way == 0 else groups - 1 - p)

    def within(r, count):
        return jnp.logical_and(r >= 0, r < count)

    def sides(way, r):
        by = delta[lax.rem(r, subs)]
        return (by > 0 if way == 0 else by < 0), by == 0

    def back_piece(r):
        q = jnp.maximum(r - lag, 0)
        return (q // subs) * subs + lax.rem(r, subs)

    for k in range(fold * cores):
        rows = enc_all[k].reshape(dialogs * key_len, feat)
        enc_pack[:, k * feat : (k + 1) * feat] = dot(to_packed[...], rows, 1, 0).astype(BF16)

    def project(k):
        product = dot(enc_pack[...], weights[k], 1, 0).astype(BF16)
        part[pl.ds(k * subs, subs)] = product.reshape(subs, piece_rows, HEAD_DIM)

    def out_copy(h):
        cols = pl.ds(pl.multiple_of(h * HEAD_DIM, HEAD_DIM), HEAD_DIM)
        return pltpu.make_async_copy(out_buf.at[h], attn_out.at[:, :, cols], out_sem.at[h])

    def half(k):
        return part[pl.ds(k * subs, subs)].reshape(packed, HEAD_DIM)

    def keep_grads(k):
        rows = dot(give_slots[...], slot_grad[...], 1, 0).astype(BF16)
        own[pl.ds(k * subs, subs)] = rows.reshape(subs, piece_rows, HEAD_DIM)

    def attend_keys(h):
        cols = pl.ds(pl.multiple_of(h * HEAD_DIM, HEAD_DIM), HEAD_DIM)
        mine = dot(take_slots[...], half(2 * h), 1, 0).astype(BF16)
        for c in range(cap):
            rows = pl.ds(c * key_len, key_len)
            live = mask[pl.ds(c, 1), :].astype(F32)
            scores = dot(mine[c * key_len : (c + 1) * key_len], q_buf[c, :, cols], 1, 1) * scale
            ok = lax.broadcasted_iota(jnp.int32, scores.shape, 0) < table[cap + c]
            unnormed = jnp.where(ok, jnp.exp(scores), 0.0)
            spare = 1.0 - table[c].astype(F32)
            attention = unnormed / (jnp.sum(unnormed, axis=0, keepdims=True) + spare)
            held[rows, :] = attention
            live_probs = (attention.astype(BF16).astype(F32) * live).astype(BF16)
            slot_grad[rows, :] = dot(live_probs, g_buf[c, :, cols], 1, 0).astype(BF16)
        keep_grads(2 * h)

    def attend_values(h):
        cols = pl.ds(pl.multiple_of(h * HEAD_DIM, HEAD_DIM), HEAD_DIM)
        mine = dot(take_slots[...], half(2 * h + 1), 1, 0).astype(BF16)
        for c in range(cap):
            rows = pl.ds(c * key_len, key_len)
            live = mask[pl.ds(c, 1), :].astype(F32)
            values = mine[c * key_len : (c + 1) * key_len]
            attention = held[rows, :]
            grad_probs = dot(values, g_buf[c, :, cols], 1, 1) * live
            out_buf[h, c] = dot(attention.astype(BF16), values, 0, 0).astype(BF16)
            grad_scores = (
                attention
                * (grad_probs - jnp.sum(attention * grad_probs, axis=0, keepdims=True))
            ).astype(BF16)
            slot_grad[rows, :] = (dot(grad_scores, q_buf[c, :, cols], 1, 0) * scale).astype(BF16)
        keep_grads(2 * h + 1)
        out_copy(h).start()

    rounds = pieces + lag
    steps = rounds + late

    def send_first(t):
        for way in range(2):

            @pl.when(jnp.logical_and(is_first(way), t < rounds))
            def _(way=way):
                forward, _ = sides(way, t)
                send[way, t] = jnp.where(
                    forward,
                    part[jnp.minimum(t, pieces - 1)].astype(F32),
                    own[back_piece(t)].astype(F32),
                ).astype(BF16)
                hop(way, t).start()

    project(0)

    @pl.loop(0, steps)
    def _(t):
        if TOP:
            send_first(t)

        for way in range(2):
            r = t - far(way)

            @pl.when(jnp.logical_and(within(r, rounds), jnp.logical_not(is_first(way))))
            def _(way=way, r=r):
                hop(way, r).wait_recv()

                @pl.when(jnp.logical_not(is_last(way)))
                def _():
                    forward, here = sides(way, r)
                    came = recv[way, r].astype(F32)
                    send[way, r] = jnp.where(
                        forward,
                        came + part[jnp.minimum(r, pieces - 1)].astype(F32),
                        jnp.where(here, own[back_piece(r)].astype(F32), came),
                    ).astype(BF16)
                    hop(way, r).start()

        whole = t - late

        @pl.when(within(whole, pieces))
        def _():
            @pl.when(p == 0)
            def _():
                part[whole] = (part[whole].astype(F32) + recv[1, whole].astype(F32)).astype(BF16)

            @pl.when(p == groups - 1)
            def _():
                part[whole] = (part[whole].astype(F32) + recv[0, whole].astype(F32)).astype(BF16)

            @pl.when(jnp.logical_and(p > 0, p < groups - 1))
            def _():
                part[whole] = (
                    part[whole].astype(F32)
                    + recv[0, whole].astype(F32)
                    + recv[1, whole].astype(F32)
                ).astype(BF16)

            k = whole // subs

            @pl.when(lax.rem(whole, 2 * subs) == subs - 1)
            def _():
                attend_keys(k // 2)

            @pl.when(lax.rem(whole, 2 * subs) == 2 * subs - 1)
            def _():
                attend_values(k // 2)

        if not TOP:
            send_first(t)

        @pl.when(jnp.logical_and(t + 1 < pieces, lax.rem(t + 1, subs) == 0))
        def _():
            project((t + 1) // subs)

        done = t - late - lag

        @pl.when(within(done, pieces))
        def _():
            r = done + lag
            back = back_piece(r)

            def collect(below, above):
                up, here = sides(0, r)
                rows = own[back].astype(F32)
                if below and above:
                    came = jnp.where(up, recv[1, r].astype(F32), recv[0, r].astype(F32))
                else:
                    came = (recv[1, r] if above else recv[0, r]).astype(F32)
                part[back] = jnp.where(here, rows, came).astype(BF16)

            @pl.when(p == 0)
            def _():
                collect(False, True)

            @pl.when(p == groups - 1)
            def _():
                collect(True, False)

            @pl.when(jnp.logical_and(p > 0, p < groups - 1))
            def _():
                collect(True, True)

            @pl.when(lax.rem(done, subs) == subs - 1)
            def _():
                k = done // subs
                acc[...] += dot(half(k), weights[k + 1 - 2 * lax.rem(k, 2)], 1, 1)

    enc_pack[...] = acc[...].astype(BF16)

    def pair_copy(z, f, i):
        m = lax.rem(core + i, cores)
        k = (z * fold + f) * others + i - 1
        return remote(
            d_send.at[f * cores + m, z], d_pair.at[k], pair_send.at[k], pair_recv.at[k],
            (section, p, m),
        )

    def paired(z, f, j):
        total = d_send[f * cores + core, z, j].astype(F32)
        for i in range(1, cores):
            total = total + d_pair[(z * fold + f) * others + i - 1, j].astype(F32)
        return total

    def term_copy(t, s, to):
        return remote(
            d_mid.at[t, to],
            d_recv.at[t, s],
            term_send.at[t * sections + to],
            term_recv.at[t * sections + s],
            (to, p, core),
        )

    @pl.loop(0, groups + 1)
    def _(k):
        @pl.when(k < groups)
        def _():
            z = near(groups - 1 - k)
            rows = pl.ds(pl.multiple_of(z * block_rows, block_rows), block_rows)
            terms = dot(from_packed[rows, :], enc_pack[...], 1, 0).astype(BF16)
            for n in range(fold * cores):
                for j in range(sections):
                    d_send[n, z, j] = terms[
                        j * chunk : (j + 1) * chunk, n * feat : (n + 1) * feat
                    ]
            for f in range(fold):
                for i in range(1, cores):
                    pair_copy(z, f, i).start()

        @pl.when(k > 0)
        def _():
            z = near(groups - k)
            for f in range(fold):
                for i in range(1, cores):
                    pair_copy(z, f, i).wait_recv()

                @pl.loop(1, sections)
                def _(i, f=f):
                    j = lax.rem(section + i, sections)
                    d_mid[z * fold + f, j] = paired(z, f, j).astype(BF16)
                    term_copy(z * fold + f, section, j).start()

    def cross(c, f, z):
        return remote(
            d_fin.at[z * fold + f],
            d_cross.at[c * fold + f],
            cross_send.at[z * fold + f],
            cross_recv.at[c * fold + f],
            (section, z, core),
        )

    @pl.loop(0, groups)
    def _(k):
        z = near(groups - 1 - k)
        for f in range(fold):
            t = z * fold + f
            total = paired(z, f, section)
            for i in range(1, sections):
                s = lax.rem(section + sections - i, sections)
                term_copy(t, s, s).wait_recv()
                total = total + d_recv[t, s].astype(F32)
            d_fin[t] = total.astype(BF16)

            @pl.when(z != p)
            def _(f=f):
                cross(p, f, z).start()

            @pl.when(z == p)
            def _(t=t):
                d_cross[t] = d_fin[t]

    def last(s, to):
        return remote(
            d_cross.at[to], d_out.at[s], last_send.at[to], last_recv.at[s], (to, p, core)
        )

    @pl.loop(0, groups)
    def _(k):
        c = near(groups - 1 - k)
        for f in range(fold):
            s = c * fold + f

            @pl.when(c != p)
            def _(f=f):
                cross(c, f, c).wait_recv()

            @pl.when(s == section)
            def _(s=s):
                d_out[s] = d_cross[s]

            @pl.when(s != section)
            def _(s=s):
                last(section, s).start()

    for j, (a, first) in enumerate(spans):

        @pl.when(section != j)
        def _(j=j):
            last(j, j).wait_recv()

        d_encoded[a, pl.ds(first, chunk), :] = d_out[j].astype(F32)

    for h in range(heads):
        out_copy(h).wait()

    @pl.loop(0, rounds)
    def _(r):
        for way in range(2):

            @pl.when(jnp.logical_not(is_last(way)))
            def _(way=way):
                hop(way, r).wait_send()

    @pl.loop(1, sections)
    def _(i):
        s = lax.rem(section + i, sections)
        scatter(section, s).wait_send()
        last(section, s).wait_send()

    @pl.loop(0, groups)
    def _(z):
        for f in range(fold):
            t = z * fold + f

            @pl.loop(1, sections)
            def _(i, f=f, t=t):
                s = lax.rem(section + i, sections)
                fan(z, f, s).wait_send()
                term_copy(t, section, s).wait_send()

            @pl.loop(0, sections)
            def _(j, f=f):
                for i in range(1, cores):
                    pass_on(j, z, f, i).wait_send()

            for i in range(1, cores):
                pair_copy(z, f, i).wait_send()

            @pl.when(z != p)
            def _(f=f, t=t):
                along(p, f, t).wait_send()
                cross(p, f, z).wait_send()


def body(dims, encoded, counts, owner, w_key, w_value, queries, grad_out, dec_mask):
    sections, groups, cores = dims
    local_count, key_len, feat = encoded.shape
    dialogs = local_count * groups
    cap, query_len, width = queries.shape[1:]
    model_rows = w_key.shape[1]
    heads = width // HEAD_DIM
    packed = packed_rows(dialogs, key_len)
    piece_rows = min(PIECE_ROWS, packed)
    subs = packed // piece_rows
    pieces = 2 * heads * subs
    rounds = pieces + lag_of(subs, groups)
    others = cores - 1
    chunk = local_count * key_len // sections
    tile = (chunk, feat)
    lanes = sections // groups * cores
    item = (piece_rows, HEAD_DIM)
    rows = dialogs * key_len
    dma = pltpu.SemaphoreType.DMA
    vmem = pl.BlockSpec(memory_space=pltpu.VMEM)
    smem = pl.BlockSpec(memory_space=pltpu.SMEM)
    hbm = pl.BlockSpec(memory_space=pl.ANY)
    attended, d_encoded = pl.pallas_call(
        functools.partial(kernel, dims),
        out_shape=(
            jax.ShapeDtypeStruct((cap, query_len, width), BF16),
            jax.ShapeDtypeStruct((local_count, key_len, feat), F32),
        ),
        in_specs=[smem, smem, vmem, hbm, hbm, hbm, hbm, vmem],
        out_specs=(hbm, vmem),
        scratch_shapes=[
            pltpu.SMEM((2 * cap,), jnp.int32),
            pltpu.VMEM((2 * heads, model_rows, HEAD_DIM), BF16),
            pltpu.VMEM((cap, query_len, width), BF16),
            pltpu.VMEM((cap, query_len, width), BF16),
            pltpu.VMEM((heads, cap, query_len, HEAD_DIM), BF16),
            pltpu.VMEM((sections,) + tile, BF16),
            pltpu.VMEM((lanes, groups, sections) + tile, BF16),
            pltpu.VMEM((packed, model_rows), BF16),
            pltpu.VMEM((packed, rows), BF16),
            pltpu.VMEM((rows, packed), BF16),
            pltpu.VMEM((cap * key_len, packed), BF16),
            pltpu.VMEM((packed, cap * key_len), BF16),
            pltpu.VMEM((subs, piece_rows, HEAD_DIM), jnp.int32),
            pltpu.VMEM((pieces,) + item, BF16),
            pltpu.VMEM((2, rounds) + item, BF16),
            pltpu.VMEM((2, rounds) + item, BF16),
            pltpu.VMEM((pieces,) + item, BF16),
            pltpu.VMEM((cap * key_len, HEAD_DIM), BF16),
            pltpu.VMEM((cap * key_len, query_len), F32),
            pltpu.VMEM((packed, model_rows), F32),
            pltpu.VMEM((lanes, groups, sections) + tile, BF16),
            pltpu.VMEM((sections * others, sections) + tile, BF16),
            pltpu.VMEM((sections, sections) + tile, BF16),
            pltpu.VMEM((sections, sections) + tile, BF16),
            pltpu.VMEM((sections,) + tile, BF16),
            pltpu.VMEM((sections,) + tile, BF16),
            pltpu.VMEM((sections,) + tile, BF16),
            pltpu.VMEM((sections,) + tile, BF16),
            dma((2 * heads,)),
            dma((2,)),
            dma((heads,)),
            dma((sections,)),
            dma((sections,)),
            dma((sections,)),
            dma((sections,)),
            dma((sections * sections,)),
            dma((sections * sections * others,)),
            dma((sections * sections * cores,)),
            dma((2, rounds)),
            dma((2, rounds)),
            dma((sections * others,)),
            dma((sections * others,)),
            dma((sections * sections,)),
            dma((sections * sections,)),
            dma((sections,)),
            dma((sections,)),
            dma((sections,)),
            dma((sections,)),
        ],
        compiler_params=pltpu.CompilerParams(
            collective_id=0, has_side_effects=True, vmem_limit_bytes=60 * 1024 * 1024
        ),
    )(counts, owner, encoded, w_key[0], w_value[0], queries[0], grad_out[0], dec_mask)
    return (attended[None], d_encoded)


def solution(mesh):
    placed = (
        P("dp", None, ("section", "mp")),
        P(),
        P(),
        P("section", "dp", "mp"),
        P("section", "dp", "mp"),
        P("section", "dp", None, "mp"),
        P("section", "dp", None, "mp"),
        P("dp", None),
    )
    dims = tuple(mesh.shape[name] for name in ("section", "dp", "mp"))
    return jax.shard_map(
        functools.partial(body, dims),
        mesh=mesh,
        in_specs=placed,
        out_specs=(P("section", "dp", None, "mp"), P("dp", None, ("section", "mp"))),
        check_vma=False,
    )
```

time: 118 us -> 103 us (0.87)
  the two profiles are of different devices: /device:TPU:3 before, /device:TPU:0 now
where the time goes in v2:
time: 103 us
  Pallas kernels  99.1 us (96%)
  local copies, waits for them, and re-layouts  3.01 us (3%)
    pallas_call x1, Pallas kernels, body(): pl.pallas_call(functools.partial(kernel, dims), out_shape=(jax.ShapeDtype...  99.1 us
    unnamed x4, local copies, waits for them, and re-layouts  3.01 us

profile of v2, /device:TPU:0, one launch (start us, length us, event | category | flops | bytes accessed | tf_op | source)
XLA Modules:
  0.0 102.8 jit_solution(7076451589823522385)
XLA Ops:
  0.6 99.1 %shard_map.95 = (bf16[4,128,1024]{2,1,0:T(8,128)(2,1)}, f32[2,64,512]{2,1,0:T(8,128)}) custom-call(s32[8]{0:T(128)} %counts.1, s32[8]{0:T(128)} %owner.1, f32[2,64,512]{2,1,0:T(8,128)} %encoded.1, bf16[1024,1024]{1,0:T(8,128)(2,1)} %bitcast.5, bf16[1024,1024]{1,0:T(8,128)(2,1)} %bitcast.6, bf16[4,128,1024]{2,1,0:T(8,128)(2,1)} %bitcast.7, ...), custom_call_target="tpu_custom_call" | custom-call | tf_op jit(solution)/shard_map/pallas_call | solution.py:689
  99.7 0.0 copy-start
  99.7 2.3 %copy.12 = bf16[1,4,128,1024]{3,2,1,0:T(8,128)(2,1)} copy(bf16[1,4,128,1024]{3,2,1,0:T(8,128)(2,1)} %bitcast.9) | data formatting | bytes 2097152
  102.0 0.0 copy-done
  102.1 0.7 copy.13
Async XLA Ops:
  99.7 2.3 %copy-start = (f32[2,64,512]{2,1,0:T(8,128)S(1)}, f32[2,64,512]{2,1,0:T(8,128)}, u32[]{:S(2)}) copy-start(f32[2,64,512]{2,1,0:T(8,128)} %get-tuple-element.9) | copy-start | bytes 786436

commit v3 on v2

--- a/solution.py
+++ b/solution.py
@@ -45,13 +45,12 @@
     queries,
     grad_out,
     mask,
-    attn_out,
-    d_encoded,
+    out_buf,
+    d_out,
     table,
     weights,
     q_buf,
     g_buf,
-    out_buf,
     enc_cast,
     enc_all,
     enc_pack,
@@ -73,11 +72,9 @@
     d_recv,
     d_fin,
     d_cross,
-    d_out,
     mid,
     w_sem,
     io_sem,
-    out_sem,
     scatter_send,
     scatter_recv,
     along_send,
@@ -352,10 +349,6 @@
         product = dot(enc_pack[...], weights[k], 1, 0).astype(BF16)
         part[pl.ds(k * subs, subs)] = product.reshape(subs, piece_rows, HEAD_DIM)
 
-    def out_copy(h):
-        cols = pl.ds(pl.multiple_of(h * HEAD_DIM, HEAD_DIM), HEAD_DIM)
-        return pltpu.make_async_copy(out_buf.at[h], attn_out.at[:, :, cols], out_sem.at[h])
-
     def half(k):
         return part[pl.ds(k * subs, subs)].reshape(packed, HEAD_DIM)
 
@@ -395,7 +388,6 @@
             ).astype(BF16)
             slot_grad[rows, :] = (dot(grad_scores, q_buf[c, :, cols], 1, 0) * scale).astype(BF16)
         keep_grads(2 * h + 1)
-        out_copy(h).start()
 
     rounds = pieces + lag
     steps = rounds + late
@@ -614,16 +606,10 @@
             def _(s=s):
                 last(section, s).start()
 
-    for j, (a, first) in enumerate(spans):
-
-        @pl.when(section != j)
-        def _(j=j):
-            last(j, j).wait_recv()
-
-        d_encoded[a, pl.ds(first, chunk), :] = d_out[j].astype(F32)
-
-    for h in range(heads):
-        out_copy(h).wait()
+    @pl.loop(1, sections)
+    def _(i):
+        j = lax.rem(section + i, sections)
+        last(j, j).wait_recv()
 
     @pl.loop(0, rounds)
     def _(r):
@@ -662,6 +648,21 @@
             def _(f=f, t=t):
                 along(p, f, t).wait_send()
                 cross(p, f, z).wait_send()
+
+
+def finish(out_buf, d_out, attn_out, d_encoded, sem):
+    heads, chunk, key_len = out_buf.shape[0], d_out.shape[1], d_encoded.shape[1]
+    copies = []
+    for h in range(heads):
+        cols = pl.ds(h * HEAD_DIM, HEAD_DIM)
+        copy = pltpu.make_async_copy(out_buf.at[h], attn_out.at[:, :, cols], sem.at[h])
+        copy.start()
+        copies.append(copy)
+    for j in range(d_out.shape[0]):
+        a, first = divmod(j * chunk, key_len)
+        d_encoded[a, pl.ds(first, chunk), :] = d_out[j].astype(F32)
+    for copy in copies:
+        copy.wait()
 
 
 def body(dims, encoded, counts, owner, w_key, w_value, queries, grad_out, dec_mask):
@@ -686,20 +687,19 @@
     vmem = pl.BlockSpec(memory_space=pltpu.VMEM)
     smem = pl.BlockSpec(memory_space=pltpu.SMEM)
     hbm = pl.BlockSpec(memory_space=pl.ANY)
-    attended, d_encoded = pl.pallas_call(
+    attended, gathered = pl.pallas_call(
         functools.partial(kernel, dims),
         out_shape=(
-            jax.ShapeDtypeStruct((cap, query_len, width), BF16),
-            jax.ShapeDtypeStruct((local_count, key_len, feat), F32),
+            pltpu.VMEM((heads, cap, query_len, HEAD_DIM), BF16),
+            pltpu.VMEM((sections,) + tile, BF16),
         ),
         in_specs=[smem, smem, vmem, hbm, hbm, hbm, hbm, vmem],
-        out_specs=(hbm, vmem),
+        out_specs=(vmem, vmem),
         scratch_shapes=[
             pltpu.SMEM((2 * cap,), jnp.int32),
             pltpu.VMEM((2 * heads, model_rows, HEAD_DIM), BF16),
             pltpu.VMEM((cap, query_len, width), BF16),
             pltpu.VMEM((cap, query_len, width), BF16),
-            pltpu.VMEM((heads, cap, query_len, HEAD_DIM), BF16),
             pltpu.VMEM((sections,) + tile, BF16),
             pltpu.VMEM((lanes, groups, sections) + tile, BF16),
             pltpu.VMEM((packed, model_rows), BF16),
@@ -722,10 +722,8 @@
             pltpu.VMEM((sections,) + tile, BF16),
             pltpu.VMEM((sections,) + tile, BF16),
             pltpu.VMEM((sections,) + tile, BF16),
-            pltpu.VMEM((sections,) + tile, BF16),
             dma((2 * heads,)),
             dma((2,)),
-            dma((heads,)),
             dma((sections,)),
             dma((sections,)),
             dma((sections,)),
@@ -748,7 +746,17 @@
             collective_id=0, has_side_effects=True, vmem_limit_bytes=60 * 1024 * 1024
         ),
     )(counts, owner, encoded, w_key[0], w_value[0], queries[0], grad_out[0], dec_mask)
-    return (attended[None], d_encoded)
+    attn_out, d_encoded = pl.pallas_call(
+        finish,
+        out_shape=(
+            jax.ShapeDtypeStruct((cap, query_len, width), BF16),
+            jax.ShapeDtypeStruct((local_count, key_len, feat), F32),
+        ),
+        in_specs=[vmem, vmem],
+        out_specs=(hbm, vmem),
+        scratch_shapes=[dma((heads,))],
+    )(*(pltpu.with_memory_space_constraint(x, pltpu.VMEM) for x in (attended, gathered)))
+    return (attn_out[None], d_encoded)
 
 
 def solution(mesh):

time: 103 us -> 101 us (0.981)
  local copies, waits for them, and re-layouts: 3.01 us -> 0 us
    unnamed x4 -> x0, local copies, waits for them, and re-layouts: 3.01 us -> none
    pallas_call x1 -> x2, Pallas kernels: 99.1 us -> 100 us  [the longest x1 98.3 us: body(): pl.pallas_call(functools.partial(kernel, dims), out_shape=(pltpu.VMEM((he...]
where the time goes in v3:
time: 101 us
  Pallas kernels  100 us (99%)
    pallas_call x1, Pallas kernels, body(): pl.pallas_call(functools.partial(kernel, dims), out_shape=(pltpu.VMEM((he...  98.3 us

profile of v3, /device:TPU:0, one launch (start us, length us, event | category | flops | bytes accessed | tf_op | source)
XLA Modules:
  0.0 100.6 jit_solution(15064695429730163554)
XLA Ops:
  0.6 98.3 %shard_map.95 = (bf16[4,4,128,256]{3,2,1,0:T(8,128)(2,1)S(1)}, bf16[4,32,512]{2,1,0:T(8,128)(2,1)S(1)}) custom-call(s32[8]{0:T(128)} %counts.1, s32[8]{0:T(128)} %owner.1, f32[2,64,512]{2,1,0:T(8,128)} %encoded.1, bf16[1024,1024]{1,0:T(8,128)(2,1)} %bitcast.5, bf16[1024,1024]{1,0:T(8,128)(2,1)} %bitcast.6, bf16[4,128,1024]{2,1,0:T(8,128)(2,1)} %bitcast.7, ...), custom_call_target="tpu_custom_call" | custom-call | tf_op jit(solution)/shard_map/pallas_call | solution.py:690
  98.9 1.7 %shard_map.96 = (bf16[4,128,1024]{2,1,0:T(8,128)(2,1)}, f32[2,64,512]{2,1,0:T(8,128)}) custom-call(bf16[4,4,128,256]{3,2,1,0:T(8,128)(2,1)S(1)} %get-tuple-element.6.out_buf, bf16[4,32,512]{2,1,0:T(8,128)(2,1)S(1)} %get-tuple-element.7.d_out), custom_call_target="tpu_custom_call" | custom-call | tf_op jit(solution)/shard_map/pallas_call | solution.py:749
